TPU v7x, 32 devices: a whole 2x2x4 slice. The times are simulated.
32 devices in a mesh: dp: 8 (over y, x, core), tensor: 4 (over z).
Axes of the slice: x: 2, y: 2, z: 4, core: 2. Of those that a mesh axis runs over, the one named last changes fastest.
Arguments:
- tokens: bfloat16 [5120, 2048], P('dp'), may hold values from -6 to 6
- cotangent: bfloat16 [5120, 2048], P('dp'), may hold values from -6 to 6
- token_slots: int32 [5120], replicated, may hold values from 0 to 8191, as said below
- lengths: int32 [8, 3], P('dp'), may hold values from 0 to 1024, as said below
- mixer_gain: bfloat16 [2048], replicated, may hold values from 0.5 to 1.5
- query_weight: bfloat16 [2048, 1024], P(None, 'tensor'), may hold values from -0.125 to 0.125
- key_weight: bfloat16 [2048, 1024], P(None, 'tensor'), may hold values from -0.125 to 0.125
- value_weight: bfloat16 [2048, 2048], P(None, 'tensor'), may hold values from -0.125 to 0.125
- gate_weight: bfloat16 [2048, 2048], P(None, 'tensor'), may hold values from -0.125 to 0.125
- decay_down: bfloat16 [2048, 16], replicated, may hold values from -0.125 to 0.125
- decay_up: bfloat16 [1024, 16], P('tensor'), may hold values from -1.5 to 1.5
- decay_bias: bfloat16 [1024], P('tensor'), may hold values from -3 to 5
- head_gain: bfloat16 [512], replicated, may hold values from 0.5 to 1.5
- out_weight: bfloat16 [2048, 2048], P('tensor'), may hold values from -0.125 to 0.125
- feed_gain: bfloat16 [2048], replicated, may hold values from 0.5 to 1.5
- feed_gate: bfloat16 [2048, 5632], P(None, 'tensor'), may hold values from -0.125 to 0.125
- feed_up: bfloat16 [2048, 5632], P(None, 'tensor'), may hold values from -0.125 to 0.125
- feed_down: bfloat16 [5632, 2048], P('tensor'), may hold values from -0.078125 to 0.078125
Outputs:
- layer_out: bfloat16 [5120, 2048], P('dp')
- token_grad: bfloat16 [5120, 2048], P('dp')
- grad_mixer_gain: float32 [2048], P('dp')
- grad_query: float32 [2048, 1024], P('dp', 'tensor')
- grad_key: float32 [2048, 1024], P('dp', 'tensor')
- grad_value: float32 [2048, 2048], P('dp', 'tensor')
- grad_gate: float32 [2048, 2048], P('dp', 'tensor')
- grad_decay_down: float32 [2048, 16], P('dp')
- grad_decay_up: float32 [4, 256, 16], P('tensor', 'dp')
- grad_decay_bias: float32 [4, 256], P('tensor', 'dp')
- grad_head_gain: float32 [512], P('dp')
- grad_out: float32 [4, 512, 2048], P('tensor', 'dp')
- grad_feed_gain: float32 [2048], P('dp')
- grad_feed_gate: float32 [2048, 5632], P('dp', 'tensor')
- grad_feed_up: float32 [2048, 5632], P('dp', 'tensor')
- grad_feed_down: float32 [4, 1408, 2048], P('tensor', 'dp')
Inputs may be any that keep to these rules, and one draw needn't show every extreme that they name: `token_slots`: the tokens of one sequence fill consecutive positions of one owner, starting at the sum of the lengths before it; every position below the sum of its owner's lengths receives exactly one token and no position above it; the last owner's positions are all filled; of the 640 tokens of one data device's block at most 128 go to one owner, and some owner receives exactly 128 from every block. The lengths of one owner sum to at most 1024, all lengths together to 5120; a length may be 0; some owner holds one sequence of 1024 tokens.
All inputs are finite; a program needn't handle non-finite values.
Results may differ from a plain program's by a relative error of at most 0.019.
Values may be sent and summed in bfloat16 or wider, within the bound.
A program may use at most 256 MiB of HBM per device.

v0:
```python
import jax
import jax.numpy as jnp
from jax import lax
from jax.sharding import PartitionSpec as P

SPAN = 64
OWN_CAP = 1024
epsilon = 1e-06
head_floor = 1.0
highest_precision = lax.Precision.HIGHEST


def segment_ids(lengths_row, row_count):
    boundary = jnp.cumsum(lengths_row)
    position = jnp.arange(row_count, dtype=jnp.int32)
    return jnp.sum((position[:, None] >= boundary[None, :]).astype(jnp.int32), axis=1)


def norm_rows(row_block, gain_row):
    return (
        row_block
        * lax.rsqrt(jnp.mean(row_block * row_block, axis=-1, keepdims=True) + epsilon)
        * gain_row
    )


def gla_head(query_rows, key_rows, value_rows, gate_logits, out_gate, head_gain, segments):
    row_count = query_rows.shape[0]
    key_width = query_rows.shape[1]
    value_width = value_rows.shape[1]
    blocks = row_count // SPAN
    log_decay = (jax.nn.log_sigmoid(gate_logits) / 16.0).reshape(blocks, SPAN, key_width)
    cumulative = jnp.cumsum(log_decay, axis=1)
    span_total = cumulative[:, SPAN - 1, :]
    queries = (query_rows * float(key_width) ** (-0.5)).reshape(blocks, SPAN, key_width)
    key_block = key_rows.reshape(blocks, SPAN, key_width)
    value_vectors = value_rows.reshape(blocks, SPAN, value_width)
    labels = segments.reshape(blocks, SPAN)
    before = jnp.concatenate([jnp.full((1,), -1, jnp.int32), labels[:-1, SPAN - 1]])
    state_carried_in = (labels == before[:, None]).astype(jnp.float32)
    tail_mask = (labels == labels[:, SPAN - 1 :]).astype(jnp.float32)
    position = jnp.arange(SPAN, dtype=jnp.int32)
    allowed = (position[None, :, None] >= position[None, None, :]) & (
        labels[:, :, None] == labels[:, None, :]
    )
    query_decay_scaled = queries * jnp.exp(cumulative)
    key_grown = key_block * jnp.exp(-cumulative)
    key_final = key_block * jnp.exp(span_total[:, None, :] - cumulative) * tail_mask[:, :, None]
    score_matrix = jnp.einsum(
        "nid,njd->nij", query_decay_scaled, key_grown, precision=highest_precision
    )
    score_matrix = jnp.where(allowed, score_matrix, 0.0)
    inside_span_part = jnp.einsum(
        "kgp,kpc->kgc", score_matrix, value_vectors, precision=highest_precision
    )
    updates = jnp.einsum("njd,nje->nde", key_final, value_vectors, precision=highest_precision)

    def advance(carry_state, inputs):
        update, decay_total, keep_flag = inputs
        return (keep_flag * jnp.exp(decay_total)[:, None] * carry_state + update, carry_state)

    _, state_entering_span = lax.scan(
        advance,
        jnp.zeros((key_width, value_width), jnp.float32),
        (updates, span_total, state_carried_in[:, SPAN - 1]),
    )
    cross_span_part = jnp.einsum(
        "rsm,rmh->rsh",
        query_decay_scaled * state_carried_in[:, :, None],
        state_entering_span,
        precision=highest_precision,
    )
    output = (inside_span_part + cross_span_part).reshape(row_count, value_width)
    scaling = lax.rsqrt(jnp.mean(output * output, axis=-1, keepdims=True) + head_floor)
    return output * scaling * head_gain * jax.nn.silu(out_gate)


def contract_rows(left_mat, right_mat):
    return lax.dot_general(
        left_mat, right_mat, (((0,), (0,)), ((), ())), preferred_element_type=jnp.float32
    )


def times_transposed(left_mat, right_mat):
    return lax.dot_general(
        left_mat, right_mat, (((1,), (1,)), ((), ())), preferred_element_type=jnp.float32
    )


def per_device(
    tokens,
    cotangent,
    token_slots,
    lengths,
    mixer_gain,
    query_weight,
    key_weight,
    value_weight,
    gate_weight,
    decay_down,
    decay_up,
    decay_bias,
    head_gain,
    out_weight,
    feed_gain,
    feed_gate,
    feed_up,
    feed_down,
):
    groups = lax.axis_size("dp")
    member = lax.axis_index("dp")
    local_count = tokens.shape[0]
    model_width = tokens.shape[1]
    peer_cap = OWN_CAP // groups
    my_slots = lax.dynamic_slice_in_dim(token_slots, member * local_count, local_count)
    my_owner = my_slots // OWN_CAP
    owner_ids = jnp.arange(groups, dtype=jnp.int32)
    chosen = (my_owner[:, None] == owner_ids[None, :]).astype(jnp.int32)
    rank_in = jnp.sum((jnp.cumsum(chosen, axis=0) - 1) * chosen, axis=1)
    send_pos = my_owner * peer_cap + rank_in

    def pack_rows(row_block):
        buffer_rows = (
            jnp.zeros((groups * peer_cap, model_width), row_block.dtype).at[send_pos].set(row_block)
        )
        return buffer_rows.reshape(groups, peer_cap, model_width)

    arrived = (
        lax.all_to_all(pack_rows(tokens), "dp", split_axis=0, concat_axis=0, tiled=True),
        lax.all_to_all(pack_rows(cotangent), "dp", split_axis=0, concat_axis=0, tiled=True),
    )
    every_owner = (token_slots // OWN_CAP).reshape(groups, local_count)
    is_mine = (every_owner == member).astype(jnp.int32)
    recv_rank = jnp.cumsum(is_mine, axis=1) - 1
    recv_index = jnp.where(
        is_mine > 0, owner_ids[:, None] * peer_cap + recv_rank, groups * peer_cap
    )
    slot_local = (token_slots % OWN_CAP).reshape(groups, local_count)
    slot_map = (
        jnp.full((groups * peer_cap + 1,), OWN_CAP, jnp.int32)
        .at[recv_index.reshape(-1)]
        .set(slot_local.reshape(-1))[: groups * peer_cap]
    )

    def place_rows(row_block):
        flat_block = row_block.reshape(groups * peer_cap, model_width)
        return (
            jnp.zeros((OWN_CAP + 1, model_width), row_block.dtype)
            .at[slot_map]
            .set(flat_block)[:OWN_CAP]
        )

    def unplace_rows(row_block):
        padded = jnp.concatenate([row_block, jnp.zeros((1, model_width), row_block.dtype)], axis=0)
        return padded[slot_map].reshape(groups, peer_cap, model_width)

    def take_back(returned):
        return returned.reshape(groups * peer_cap, model_width)[send_pos]

    owner_rows = place_rows(arrived[0]).astype(jnp.float32)
    upstream = place_rows(arrived[1])
    labels = segment_ids(lengths[0], OWN_CAP)
    mixed_wide, mixer_norm_back = jax.vjp(norm_rows, owner_rows, mixer_gain.astype(jnp.float32))
    normed = mixed_wide.astype(jnp.bfloat16)

    def project(weight):
        return jnp.dot(normed, weight, preferred_element_type=jnp.float32)

    queries = project(query_weight).astype(jnp.bfloat16)
    keys_low = project(key_weight).astype(jnp.bfloat16)
    value_vectors = project(value_weight).astype(jnp.bfloat16)
    gate_pre = project(gate_weight)
    latent = project(decay_down)
    decay_up_wide = decay_up.astype(jnp.float32)
    logits = lax.dot_general(
        latent, decay_up_wide, (((1,), (1,)), ((), ())), precision=highest_precision
    ) + decay_bias.astype(jnp.float32)

    def mixer(query_wide, key_wide, value_wide, logit_wide, gate_wide, gain_wide):
        return gla_head(query_wide, key_wide, value_wide, logit_wide, gate_wide, gain_wide, labels)

    gated_wide, mixer_back = jax.vjp(
        mixer,
        queries.astype(jnp.float32),
        keys_low.astype(jnp.float32),
        value_vectors.astype(jnp.float32),
        logits,
        gate_pre,
        head_gain.astype(jnp.float32),
    )
    gated_low = gated_wide.astype(jnp.bfloat16)
    mixer_partial = jnp.dot(gated_low, out_weight, preferred_element_type=jnp.float32)
    hidden = owner_rows + lax.psum(mixer_partial, "tensor")
    feed_wide, feed_norm_back = jax.vjp(norm_rows, hidden, feed_gain.astype(jnp.float32))
    feed_normed = feed_wide.astype(jnp.bfloat16)
    gate_hidden = jnp.dot(feed_normed, feed_gate, preferred_element_type=jnp.float32)
    up_hidden = jnp.dot(feed_normed, feed_up, preferred_element_type=jnp.float32)
    sigmoid_gate = jax.nn.sigmoid(gate_hidden)
    swish_gate = gate_hidden * sigmoid_gate
    active = (swish_gate * up_hidden).astype(jnp.bfloat16)
    feed_partial = jnp.dot(active, feed_down, preferred_element_type=jnp.float32)
    layer_rows = (
        hidden + lax.psum(feed_partial.astype(jnp.bfloat16), "tensor").astype(jnp.float32)
    ).astype(jnp.bfloat16)
    upstream_wide = upstream.astype(jnp.float32)
    grad_feed_down = contract_rows(active, upstream)
    d_active = times_transposed(upstream, feed_down)
    d_gate_hidden = (
        d_active * up_hidden * sigmoid_gate * (1.0 + gate_hidden * (1.0 - sigmoid_gate))
    ).astype(jnp.bfloat16)
    d_up_hidden = (d_active * swish_gate).astype(jnp.bfloat16)
    grad_feed_gate = contract_rows(feed_normed, d_gate_hidden)
    grad_feed_up = contract_rows(feed_normed, d_up_hidden)
    feed_part = times_transposed(d_gate_hidden, feed_gate) + times_transposed(d_up_hidden, feed_up)
    d_feed = lax.psum(feed_part, "tensor")
    d_hidden_norm, grad_feed_gain = feed_norm_back(d_feed)
    d_hidden = upstream_wide + d_hidden_norm
    d_mixed = d_hidden.astype(jnp.bfloat16)
    gain_term = jnp.zeros((model_width,), jnp.float32)
    grad_out = contract_rows(gated_low, d_mixed)
    d_gated = times_transposed(d_mixed, out_weight)
    d_query, d_key, d_value, d_logits, d_gate, d_head_gain = mixer_back(d_gated)
    d_query_low = d_query.astype(jnp.bfloat16)
    d_key_low = d_key.astype(jnp.bfloat16)
    d_value_low = d_value.astype(jnp.bfloat16)
    d_gate_low = d_gate.astype(jnp.bfloat16)
    grad_decay_bias = jnp.sum(d_logits, axis=0)
    grad_decay_up = lax.dot_general(
        d_logits, latent, (((0,), (0,)), ((), ())), precision=highest_precision
    )
    latent_part = jnp.dot(d_logits, decay_up_wide, precision=highest_precision)
    mixer_part = (
        times_transposed(d_query_low, query_weight)
        + times_transposed(d_key_low, key_weight)
        + times_transposed(d_value_low, value_weight)
        + times_transposed(d_gate_low, gate_weight)
    )
    summed = lax.psum((mixer_part, latent_part, d_head_gain, gain_term), "tensor")
    d_latent = summed[1]
    d_normed = summed[0] + lax.dot_general(
        d_latent,
        decay_down.astype(jnp.float32),
        (((1,), (1,)), ((), ())),
        precision=highest_precision,
    )
    grad_decay_down = lax.dot_general(
        normed.astype(jnp.float32), d_latent, (((0,), (0,)), ((), ())), precision=highest_precision
    )
    grad_query = contract_rows(normed, d_query_low)
    grad_key = contract_rows(normed, d_key_low)
    grad_value = contract_rows(normed, d_value_low)
    grad_gate = contract_rows(normed, d_gate_low)
    d_rows_norm, grad_mixer_gain = mixer_norm_back(d_normed)
    token_rows = (d_hidden + d_rows_norm).astype(jnp.bfloat16)
    shares = (
        lax.psum_scatter(grad_mixer_gain, "dp", scatter_dimension=0, tiled=True),
        lax.psum_scatter(grad_query, "dp", scatter_dimension=0, tiled=True),
        lax.psum_scatter(grad_key, "dp", scatter_dimension=0, tiled=True),
        lax.psum_scatter(grad_value, "dp", scatter_dimension=0, tiled=True),
        lax.psum_scatter(grad_gate, "dp", scatter_dimension=0, tiled=True),
        lax.psum_scatter(grad_decay_down, "dp", scatter_dimension=0, tiled=True),
        lax.psum_scatter(grad_decay_up, "dp", scatter_dimension=0, tiled=True),
        lax.psum_scatter(grad_decay_bias, "dp", scatter_dimension=0, tiled=True),
        lax.psum_scatter(summed[2], "dp", scatter_dimension=0, tiled=True),
        lax.psum_scatter(grad_out, "dp", scatter_dimension=0, tiled=True),
        lax.psum_scatter(grad_feed_gain, "dp", scatter_dimension=0, tiled=True),
        lax.psum_scatter(grad_feed_gate, "dp", scatter_dimension=0, tiled=True),
        lax.psum_scatter(grad_feed_up, "dp", scatter_dimension=0, tiled=True),
        lax.psum_scatter(grad_feed_down, "dp", scatter_dimension=0, tiled=True),
    )
    returned = (
        lax.all_to_all(unplace_rows(layer_rows), "dp", split_axis=0, concat_axis=0, tiled=True),
        lax.all_to_all(unplace_rows(token_rows), "dp", split_axis=0, concat_axis=0, tiled=True),
    )
    layer_out = take_back(returned[0])
    token_grad = take_back(returned[1])
    rank_width = decay_up.shape[1]
    return (
        layer_out,
        token_grad,
        shares[0],
        shares[1],
        shares[2],
        shares[3],
        shares[4],
        shares[5],
        shares[6].reshape(1, -1, rank_width),
        shares[7].reshape(1, -1),
        shares[8],
        shares[9].reshape(1, shares[9].shape[0], model_width),
        shares[10],
        shares[11],
        shares[12],
        shares[13].reshape(1, shares[13].shape[0], model_width),
    )


def solution(mesh):
    placed = (
        P("dp", None),
        P("dp", None),
        P(),
        P("dp", None),
        P(),
        P(None, "tensor"),
        P(None, "tensor"),
        P(None, "tensor"),
        P(None, "tensor"),
        P(),
        P("tensor", None),
        P("tensor"),
        P(),
        P("tensor", None),
        P(),
        P(None, "tensor"),
        P(None, "tensor"),
        P("tensor", None),
    )
    return jax.shard_map(
        per_device,
        mesh=mesh,
        in_specs=placed,
        out_specs=(
            P("dp", None),
            P("dp", None),
            P("dp"),
            P("dp", "tensor"),
            P("dp", "tensor"),
            P("dp", "tensor"),
            P("dp", "tensor"),
            P("dp", None),
            P("tensor", "dp", None),
            P("tensor", "dp"),
            P("dp"),
            P("tensor", "dp", None),
            P("dp"),
            P("dp", "tensor"),
            P("dp", "tensor"),
            P("tensor", "dp", None),
        ),
        check_vma=False,
    )
```

profile of v0, /device:TPU:0, one launch (start us, length us, event | category | flops | bytes accessed | tf_op | source)
XLA Modules:
  0.0 2135.5 jit_solution(18394428422442927344)
XLA Ops:
  11.7 10.5 scatter_custom_fusion.1
  22.2 5.3 all-to-all-start
  30.1 19.2 scatter_custom_fusion
  50.7 26.0 %all-to-all-done = bf16[8,128,2048]{2,1,0:T(8,128)(2,1)} async-done(((bf16[8,128,2048]{2,1,0:T(8,128)(2,1)}), bf16[8,128,2048]{2,1,0:T(8,128)(2,1)}, u32[]{:S(2)}, u32[]{:S(2)}) %all-to-all-start) | async-done | bytes 4194336 | tf_op jit(solution)/shard_map/all_to_all | solution.py:129
  76.7 10.1 scatter_custom_fusion.2
  109.0 6.7 fusion.66
  120.0 61.8 %while.36 = (s32[]{:T(128)}, f32[256,512]{1,0:T(8,128)S(1)}, f32[16,256,512]{2,1,0:T(8,128)}, f32[16,256]{1,0:T(8,128)S(1)}, f32[16,256,1]{1,2,0:T(1,128)}, /*in...) while((s32[]{:T(128)}, f32[256,512]{1,0:T(8,128)S(1)}, ...), condition=%wide.region_13.14_spmd.clone, body=%wide.region_12.13_spmd.clone.sunk | while | flops 524547 | bytes 2629268 | solution.py:62
  182.4 10.8 multiply_reduce_fusion.4
  193.3 6.9 multiply_convert_fusion.4
  201.2 5.6 fusion.85
  206.8 10.9 scatter_custom_fusion.3
  217.7 4.7 all-to-all-start.2
  222.5 49.1 %all-to-all-done.2 = bf16[8,128,2048]{2,1,0:T(8,128)(2,1)} async-done(((bf16[8,128,2048]{2,1,0:T(8,128)(2,1)}), bf16[8,128,2048]{2,1,0:T(8,128)(2,1)}, u32[]{:S(2)}, u32[]{:S(2)}) %all-to-all-start.2) | async-done | bytes 4194336 | tf_op jit(solution)/shard_map/all_to_all | solution.py:130
  271.5 10.1 scatter_custom_fusion.4
  281.6 216.3 %all-reduce.14.cloned.1.call-done = f32[1024,2048]{1,0:T(8,128)} async-done(((f32[1024,2048]{1,0:T(8,128)}), f32[1024,2048]{1,0:T(8,128)}) %all-reduce.14.cloned.1.call-update) | async-done | bytes 8388624 | tf_op jit(solution)/shard_map/psum | solution.py:193
  497.9 5.5 multiply_reduce_fusion.2
  506.7 11.9 fusion.87
  518.6 10.3 fusion.86
  528.9 15.1 multiply_convert_fusion.1
  544.0 10.2 fusion.88
  554.2 10.9 convolution_add_fusion.1
  565.2 10.9 convolution_convert_fusion
  576.2 278.9 %all-reduce.18.cloned.1.call-done = f32[1024,2048]{1,0:T(8,128)} async-done(((f32[1024,2048]{1,0:T(8,128)}), f32[1024,2048]{1,0:T(8,128)}) %all-reduce.18.cloned.1.call-update) | async-done | bytes 8388624 | tf_op jit(solution)/shard_map/psum | solution.py:215
  855.1 7.6 multiply_reduce_fusion
  862.7 148.8 %all-reduce.16.cloned.1.call-done = bf16[1024,2048]{1,0:T(8,128)(2,1)} async-done(((bf16[1024,2048]{1,0:T(8,128)(2,1)}), bf16[1024,2048]{1,0:T(8,128)(2,1)}) %all-reduce.16.cloned.1.call-update) | async-done | bytes 4194320 | tf_op jit(solution)/shard_map/psum | solution.py:203
  1011.5 12.5 fusion.6
  1024.0 6.9 multiply_reduce_fusion.3
  1037.5 9.8 fusion.57
  1049.1 9.4 fusion.34
  1058.4 5.7 fusion.92
  1068.5 78.5 %while.37 = (s32[]{:T(128)}, f32[256,512]{1,0:T(8,128)S(1)}, f32[16,256,512]{2,1,0:T(8,128)}, f32[16,256]{1,0:T(8,128)S(1)}, f32[16,256,512]{2,1,0:T(8,128)}, /*...) while((s32[]{:T(128)}, f32[256,512]{1,0:T(8,128)S(1)}, ...), condition=%wide.region_25.26_spmd.clone, body=%wide.region_23.25_spmd.clone.sunk | while | flops 786692 | bytes 3157176 | solution.py:62
  1147.0 8.5 fusion.62
  1155.6 5.9 add_convert_fusion.1
  1169.4 5.6 fusion.91
  1177.4 9.1 add_add_fusion.2
  1189.8 5.7 fusion.94
  1195.7 4.9 fusion.93
  1200.8 7.8 fusion.24
  1209.9 6.7 fusion.96
  1217.8 6.6 fusion.95
  1224.4 254.9 %all-reduce.20.cloned.1.call-done = (f32[1024,2048]{1,0:T(8,128)}, f32[1024,16]{0,1:T(8,128)}) async-done(((f32[1024,2048]{1,0:T(8,128)}, f32[1024,16]{0,1:T(8,128)}), (f32[1024,2048]{1,0:T(8,128)}, f32[1024,16]{0,1:T(8,128)})) %all-reduce.20.cloned.1.call-update) | async-done | bytes 8454160 | tf_op jit(solution)/shard_map/psum | solution.py:238
  1479.3 4.6 fusion.97
  1484.0 11.4 fusion.12
  1495.6 11.9 fusion.99
  1507.6 11.9 fusion.98
  1519.5 4.8 concatenate.10
  1524.3 11.8 gather_fusion
  1536.1 4.9 all-to-all-start.1
  1541.1 8.8 fusion.5
  1553.7 4.7 concatenate.11
  1558.4 11.6 gather_fusion.2
  1570.0 26.1 %all-to-all-done.1 = bf16[8,128,2048]{2,1,0:T(8,128)(2,1)} async-done(((bf16[8,128,2048]{2,1,0:T(8,128)(2,1)}), bf16[8,128,2048]{2,1,0:T(8,128)(2,1)}, u32[]{:S(2)}, u32[]{:S(2)}) %all-to-all-start.1) | async-done | bytes 4194336 | tf_op jit(solution)/shard_map/all_to_all | solution.py:272
  1596.1 4.7 all-to-all-start.3
  1604.9 9.7 gather_fusion.1
  1614.6 60.6 %all-reduce.7 = (f32[2048]{0:T(1024)S(1)}, f32[256]{0:T(256)S(1)}, f32[512]{0:T(512)S(1)}, f32[2048]{0:T(1024)S(1)}) all-reduce(f32[2048]{0:T(1024)S(1)} %get-tuple-element.304, f32[256]{0:T(256)S(1)} %neg.53, f32[512]{0:T(512)S(1)} %copy-done.70, f32[2048]{0:T(1024)S(1)} %copy-done.62), channel_id=2, replica_groups=mesh['dp'=8,'tensor'=4] {'dp'}, use_global_device_ids=true, to_apply=%region_32.33.clone | all-reduce | flops 4864 | bytes 38912
  1676.5 12.4 psum.48
  1689.5 9.9 gather_fusion.3
  1699.4 8.6 reduce-scatter.23.cloned.1.call-done
  1708.0 55.7 %reduce-scatter.19.cloned.1.call-done = f32[256,512]{1,0:T(8,128)} async-done(((f32[2048,512]{1,0:T(8,128)}), f32[256,512]{1,0:T(8,128)}) %reduce-scatter.19.cloned.1.call-update) | async-done | bytes 524304 | tf_op jit(solution)/shard_map/reduce_scatter | solution.py:260
  1763.7 55.1 %reduce-scatter.17.cloned.1.call-done = f32[256,512]{1,0:T(8,128)} async-done(((f32[2048,512]{1,0:T(8,128)}), f32[256,512]{1,0:T(8,128)}) %reduce-scatter.17.cloned.1.call-update) | async-done | bytes 524304 | tf_op jit(solution)/shard_map/reduce_scatter | solution.py:259
  1818.8 37.3 %reduce-scatter.21.cloned.1.call-done = f32[256,16]{0,1:T(8,128)} async-done(((f32[2048,16]{0,1:T(8,128)}), f32[256,16]{0,1:T(8,128)}) %reduce-scatter.21.cloned.1.call-update) | async-done | bytes 16400 | tf_op jit(solution)/shard_map/reduce_scatter | solution.py:261
  1856.0 90.8 %reduce-scatter.29.cloned.1.call-done = f32[176,2048]{1,0:T(8,128)} async-done(((f32[1408,2048]{1,0:T(8,128)}), f32[176,2048]{1,0:T(8,128)}) %reduce-scatter.29.cloned.1.call-update) | async-done | bytes 1441808 | tf_op jit(solution)/shard_map/reduce_scatter | solution.py:269
  1946.8 90.9 %reduce-scatter.27.cloned.1.call-done = f32[256,1408]{1,0:T(8,128)} async-done(((f32[2048,1408]{1,0:T(8,128)}), f32[256,1408]{1,0:T(8,128)}) %reduce-scatter.27.cloned.1.call-update) | async-done | bytes 1441808 | tf_op jit(solution)/shard_map/reduce_scatter | solution.py:268
  2037.7 90.8 %reduce-scatter.25.cloned.1.call-done = f32[256,1408]{1,0:T(8,128)} async-done(((f32[2048,1408]{1,0:T(8,128)}), f32[256,1408]{1,0:T(8,128)}) %reduce-scatter.25.cloned.1.call-update) | async-done | bytes 1441808 | tf_op jit(solution)/shard_map/reduce_scatter | solution.py:267
  (500 shorter events, 215.6 us)
Async XLA Ops:
  7.2 186.1 %copy-start = (bf16[2048,512]{1,0:T(8,128)(2,1)S(1)}, bf16[2048,512]{1,0:T(8,128)(2,1)}, u32[]{:S(2)}) copy-start(bf16[2048,512]{1,0:T(8,128)(2,1)} %param.30) | copy-start | bytes 6291460
  11.7 195.1 %copy-start.64 = (s32[640]{0:T(1024)}, s32[640]{0:T(1024)S(1)}, u32[]{:S(2)}) copy-start(s32[640]{0:T(1024)S(1)} %compare_select_fusion.4) | copy-start | bytes 7684
  22.2 54.5 %all-to-all-start = ((bf16[8,128,2048]{2,1,0:T(8,128)(2,1)}), bf16[8,128,2048]{2,1,0:T(8,128)(2,1)}, u32[]{:S(2)}, u32[]{:S(2)}) async-start(bf16[8,128,2048]{2,1,0:T(8,128)(2,1)} %bitcast.199), calls=%async_computation | async-start | bytes 8388608 | tf_op jit(solution)/shard_map/all_to_all | solution.py:129
  27.5 470.4 %all-reduce.14.cloned.1.call-start = ((), (), s32[]{:S(2)}) async-start(), calls=%async_computation.14 | async-start | bytes 16777216 | tf_op jit(solution)/shard_map/psum | solution.py:193
  28.0 76.0 %copy-start.41 = (s32[16,64]{1,0:T(8,128)}, s32[16,64]{1,0:T(8,128)S(1)}, u32[]{:S(2)}) copy-start(s32[16,64]{1,0:T(8,128)S(1)} %eq.92) | copy-start | bytes 12292
  28.0 62.0 %copy-start.51 = (f32[2048]{0:T(1024)}, f32[2048]{0:T(1024)S(1)}, u32[]{:S(2)}) copy-start(f32[2048]{0:T(1024)S(1)} %convert_element_type.127) | copy-start | bytes 24580
  49.7 54.3 %copy-start.55 = (pred[64,64]{1,0:T(8,128)(4,1)}, pred[64,64]{1,0:T(8,128)(4,1)S(1)}, u32[]{:S(2)}) copy-start(pred[64,64]{1,0:T(8,128)(4,1)S(1)} %iota_compare_fusion) | copy-start | bytes 12292
  49.9 59.0 %copy-start.53 = (f32[16,64]{1,0:T(8,128)}, f32[16,64]{1,0:T(8,128)S(1)}, u32[]{:S(2)}) copy-start(f32[16,64]{1,0:T(8,128)S(1)} %get-tuple-element.369) | copy-start | bytes 12292
  96.7 12.3 copy-start.12
  99.0 9.9 copy-start.15
  106.6 9.0 copy-start.19
  182.4 10.8 copy-start.43
  182.4 10.8 copy-start.72
  193.3 7.9 copy-start.74
  217.7 53.8 %all-to-all-start.2 = ((bf16[8,128,2048]{2,1,0:T(8,128)(2,1)}), bf16[8,128,2048]{2,1,0:T(8,128)(2,1)}, u32[]{:S(2)}, u32[]{:S(2)}) async-start(bf16[8,128,2048]{2,1,0:T(8,128)(2,1)} %bitcast.200), calls=%async_computation.2 | async-start | bytes 8388608 | tf_op jit(solution)/shard_map/all_to_all | solution.py:130
  222.4 632.7 %all-reduce.18.cloned.1.call-start = ((), (), s32[]{:S(2)}) async-start(), calls=%async_computation.16 | async-start | bytes 16777216 | tf_op jit(solution)/shard_map/psum | solution.py:215
  506.7 11.9 copy-start.23
  506.7 22.2 %slice-start.6 = ((s8[4227072]{0:T(1024)(128)(4,1)}), s8[4194304]{0:T(1024)(128)(4,1)S(1)}, s32[]{:S(2)}) async-start(s8[4227072]{0:T(1024)(128)(4,1)} %bitcast.191), calls=%async_computation.34 | async-start | bytes 8388608
  518.6 10.3 slice-start.7
  544.0 10.2 copy-start.80
  565.1 446.4 %all-reduce.16.cloned.1.call-start = ((), (), s32[]{:S(2)}) async-start(), calls=%async_computation.15 | async-start | bytes 8388608 | tf_op jit(solution)/shard_map/psum | solution.py:203
  576.1 903.2 %all-reduce.20.cloned.1.call-start = ((), (), s32[]{:S(2)}) async-start(), calls=%async_computation.27 | async-start | bytes 16908288 | tf_op jit(solution)/shard_map/psum | solution.py:238
  1011.5 12.5 copy-start.18
  1011.5 12.5 copy-start.30
  1024.0 7.0 copy-start.4
  1032.9 25.5 %copy-start.34 = (bf16[1024,512]{1,0:T(8,128)(2,1)}, bf16[1024,512]{1,0:T(8,128)(2,1)S(1)}, u32[]{:S(2)}) copy-start(bf16[1024,512]{1,0:T(8,128)(2,1)S(1)} %get-tuple-element.363) | copy-start | bytes 3145732
  1033.0 16.1 slice-start.2
  1034.2 13.2 copy-start.21
  1037.5 9.8 copy-start.6
  1037.5 9.8 copy-start.13
  1037.5 11.5 slice-start.3
  1068.5 78.5 %copy-start.14 = (bf16[1024,256]{1,0:T(8,128)(2,1)S(1)}, bf16[1024,256]{1,0:T(8,128)(2,1)}, u32[]{:S(2)}) copy-start(bf16[1024,256]{1,0:T(8,128)(2,1)} %copy-done.12) | copy-start | bytes 1572868
  1068.5 78.5 %copy-start.44 = (f32[16,256]{1,0:T(8,128)S(1)}, f32[16,256]{1,0:T(8,128)}, u32[]{:S(2)}) copy-start(f32[16,256]{1,0:T(8,128)} %copy-done.43) | copy-start | bytes 49156
  1068.5 78.5 %copy-start.54 = (f32[16,64]{1,0:T(8,128)S(1)}, f32[16,64]{1,0:T(8,128)}, u32[]{:S(2)}) copy-start(f32[16,64]{1,0:T(8,128)} %copy-done.53) | copy-start | bytes 12292
  1147.0 8.6 copy-start.3
  1147.0 8.6 copy-start.17
  1155.6 6.0 copy-start.11
  1155.6 6.0 copy-start.22
  1155.6 6.0 copy-start.25
  1155.6 6.0 copy-start.26
  1161.6 7.8 copy-start.39
  1164.7 10.4 copy-start.27
  1169.4 6.9 slice-start.8
  1186.5 417.0 %reduce-scatter.31.cloned.1.call-start = ((), (), s32[]{:S(2)}) async-start(), calls=%async_computation.26 | async-start | bytes 147456
  1189.8 509.6 %reduce-scatter.15.cloned.1.call-start = ((), (), s32[]{:S(2)}) async-start(), calls=%async_computation.18 | async-start | bytes 2359296 | tf_op jit(solution)/shard_map/reduce_scatter | solution.py:258
  1195.6 503.8 %reduce-scatter.13.cloned.1.call-start = ((), (), s32[]{:S(2)}) async-start(), calls=%async_computation.17 | async-start | bytes 2359296 | tf_op jit(solution)/shard_map/reduce_scatter | solution.py:257
  1200.6 507.4 %reduce-scatter.23.cloned.1.call-start = ((), (), s32[]{:S(2)}) async-start(), calls=%async_computation.22 | async-start | bytes 4718592 | tf_op jit(solution)/shard_map/reduce_scatter | solution.py:265
  1208.7 555.0 %reduce-scatter.19.cloned.1.call-start = ((), (), s32[]{:S(2)}) async-start(), calls=%async_computation.20 | async-start | bytes 4718592 | tf_op jit(solution)/shard_map/reduce_scatter | solution.py:260
  1216.6 602.2 %reduce-scatter.17.cloned.1.call-start = ((), (), s32[]{:S(2)}) async-start(), calls=%async_computation.19 | async-start | bytes 4718592 | tf_op jit(solution)/shard_map/reduce_scatter | solution.py:259
  1224.4 631.7 %reduce-scatter.21.cloned.1.call-start = ((), (), s32[]{:S(2)}) async-start(), calls=%async_computation.21 | async-start | bytes 147456 | tf_op jit(solution)/shard_map/reduce_scatter | solution.py:261
  1483.9 462.9 %reduce-scatter.29.cloned.1.call-start = ((), (), s32[]{:S(2)}) async-start(), calls=%async_computation.25 | async-start | bytes 12976128 | tf_op jit(solution)/shard_map/reduce_scatter | solution.py:269
  1495.4 542.3 %reduce-scatter.27.cloned.1.call-start = ((), (), s32[]{:S(2)}) async-start(), calls=%async_computation.24 | async-start | bytes 12976128 | tf_op jit(solution)/shard_map/reduce_scatter | solution.py:268
  1507.6 620.9 %reduce-scatter.25.cloned.1.call-start = ((), (), s32[]{:S(2)}) async-start(), calls=%async_computation.23 | async-start | bytes 12976128 | tf_op jit(solution)/shard_map/reduce_scatter | solution.py:267
  1536.1 13.8 slice-start
  1536.1 60.0 %all-to-all-start.1 = ((bf16[8,128,2048]{2,1,0:T(8,128)(2,1)}), bf16[8,128,2048]{2,1,0:T(8,128)(2,1)}, u32[]{:S(2)}, u32[]{:S(2)}) async-start(bf16[8,128,2048]{2,1,0:T(8,128)(2,1)} %bitcast.198), calls=%async_computation.1 | async-start | bytes 8388608 | tf_op jit(solution)/shard_map/all_to_all | solution.py:272
  1541.0 8.9 slice-start.4
  1541.1 8.8 copy-start.61
  1541.1 8.9 slice-start.1
  1541.1 8.9 slice-start.5
  1596.1 7.3 copy-start.65
  1596.1 93.4 %all-to-all-start.3 = ((bf16[8,128,2048]{2,1,0:T(8,128)(2,1)}), bf16[8,128,2048]{2,1,0:T(8,128)(2,1)}, u32[]{:S(2)}, u32[]{:S(2)}) async-start(bf16[8,128,2048]{2,1,0:T(8,128)(2,1)} %bitcast.197), calls=%async_computation.3 | async-start | bytes 8388608 | tf_op jit(solution)/shard_map/all_to_all | solution.py:273
  1604.9 9.7 copy-start.62
  1604.9 9.7 copy-start.70
  1689.5 438.9 %copy-start.1 = (bf16[2048,512]{1,0:T(8,128)(2,1)S(1)}, bf16[2048,512]{1,0:T(8,128)(2,1)}, u32[]{:S(2)}) copy-start(bf16[2048,512]{1,0:T(8,128)(2,1)} %param.30) | copy-start | bytes 6291460
  (45 other events, 163.2 us)
Sparse Core Ops, SparseCore 0:
  206.9 290.9 all-reduce.13
  565.2 289.8 all-reduce.17
  857.5 153.9 all-reduce.15
  1186.6 292.6 all-reduce.19
  1482.4 32.3 reduce-scatter.30
  1518.5 60.9 reduce-scatter.14
  1583.7 69.8 reduce-scatter.12
  1657.5 50.4 reduce-scatter.22
  1712.3 51.3 reduce-scatter.18
  1767.4 51.2 reduce-scatter.16
  1822.6 33.3 reduce-scatter.20
  1859.9 86.8 reduce-scatter.28
  1950.9 86.7 reduce-scatter.26
  2041.6 86.7 reduce-scatter.24
where the time goes:
time: 2150 us; the launch traced here: 2140 us
  waiting for transfers between devices  1430 us (67%)
  matrix products  267 us (12%)
  local copies, waits for them, and re-layouts  168 us (8%)
  other arithmetic  159 us (7%)
  blocking collectives  73 us (3%)
    psum x1, waiting for transfers between devices, per_device(): d_feed = lax.psum(feed_part, 'tensor')  279 us
    psum x1, waiting for transfers between devices, per_device(): lax.psum((mixer_part, latent_part, d_head_gain, gain_term), 'tensor')  255 us
    psum x1, waiting for transfers between devices, per_device(): hidden = owner_rows + lax.psum(mixer_partial, 'tensor')  216 us
    psum x1, waiting for transfers between devices, per_device(): lax.psum(feed_partial.astype(jnp.bfloat16), 'tensor').astype(jnp.float32)  149 us
    reduce_scatter x1, waiting for transfers between devices, per_device(): lax.psum_scatter(grad_feed_up, 'dp', scatter_dimension=0, tiled=True)  90.9 us
    reduce_scatter x1, waiting for transfers between devices, per_device(): lax.psum_scatter(grad_feed_down, 'dp', scatter_dimension=0, tiled=True)  90.8 us
    reduce_scatter x1, waiting for transfers between devices, per_device(): lax.psum_scatter(grad_feed_gate, 'dp', scatter_dimension=0, tiled=True)  90.8 us
    dot_general x8, matrix products, contract_rows(): lax.dot_general(left_mat, right_mat, (((0,), (0,)), ((), ())), preferred_...  66.8 us
  transfers between devices with their start and end apart: 18, of which 14 were waited for; matrix products, arithmetic and copies ran while one was open for 10% of the time, Pallas kernels for 0%

commit v1 on v0

--- a/solution.py
+++ b/solution.py
@@ -200,7 +200,10 @@
     active = (swish_gate * up_hidden).astype(jnp.bfloat16)
     feed_partial = jnp.dot(active, feed_down, preferred_element_type=jnp.float32)
     layer_rows = (
-        hidden + lax.psum(feed_partial.astype(jnp.bfloat16), "tensor").astype(jnp.float32)
+        hidden
+        + lax.all_gather(feed_partial.astype(jnp.bfloat16), "tensor")
+        .sum(axis=0)
+        .astype(jnp.float32)
     ).astype(jnp.bfloat16)
     upstream_wide = upstream.astype(jnp.float32)
     grad_feed_down = contract_rows(active, upstream)

time: 2150 us -> 2260 us (1.051)
  waiting for transfers between devices: 1430 us -> 1530 us
    all_gather x0 -> x1, waiting for transfers between devices: none -> 279 us  [per_device(): lax.all_gather(feed_partial.astype(jnp.bfloat16), 'tensor').sum(axis=0)]
    psum x1 -> x0, waiting for transfers between devices: 149 us -> none  [per_device(): lax.psum(feed_partial.astype(jnp.bfloat16), 'tensor').astype(jnp.float32)]
    reduce_scatter x1, waiting for transfers between devices: 90.8 us -> 3.76 us  [per_device(): lax.psum_scatter(grad_feed_down, 'dp', scatter_dimension=0, tiled=True)]
    psum x1, waiting for transfers between devices: 255 us -> 198 us  [per_device(): lax.psum((mixer_part, latent_part, d_head_gain, gain_term), 'tensor')]
    reduce_scatter x1, waiting for transfers between devices: 8.56 us -> 55.7 us  [per_device(): lax.psum_scatter(grad_out, 'dp', scatter_dimension=0, tiled=True)]
    reduce_scatter x1, waiting for transfers between devices: 0.01 us -> 45.4 us  [per_device(): lax.psum_scatter(grad_key, 'dp', scatter_dimension=0, tiled=True)]
    reduce_scatter x1, waiting for transfers between devices: 0.01 us -> 44.9 us  [per_device(): lax.psum_scatter(grad_query, 'dp', scatter_dimension=0, tiled=True)]
    all_to_all x1, waiting for transfers between devices: 26.1 us -> 0.01 us  [per_device(): lax.all_to_all(unplace_rows(layer_rows), 'dp', split_axis=0, concat_axis=...]
  transfers between devices with their start and end apart: 18 -> 18, of which waited for: 14 -> 15; matrix products, arithmetic and copies ran while one was open for 10% -> 9% of each run, Pallas kernels for 0% -> 0%
where the time goes in v1:
time: 2260 us; the launch traced here: 2240 us
  waiting for transfers between devices  1530 us (68%)
  matrix products  267 us (12%)
  other arithmetic  171 us (8%)
  local copies, waits for them, and re-layouts  167 us (7%)
  blocking collectives  69.9 us (3%)
    all_gather x1, waiting for transfers between devices, per_device(): lax.all_gather(feed_partial.astype(jnp.bfloat16), 'tensor').sum(axis=0)  279 us
    psum x1, waiting for transfers between devices, per_device(): d_feed = lax.psum(feed_part, 'tensor')  279 us
    psum x1, waiting for transfers between devices, per_device(): hidden = owner_rows + lax.psum(mixer_partial, 'tensor')  216 us
    psum x1, waiting for transfers between devices, per_device(): lax.psum((mixer_part, latent_part, d_head_gain, gain_term), 'tensor')  198 us
    reduce_scatter x1, waiting for transfers between devices, per_device(): lax.psum_scatter(grad_feed_up, 'dp', scatter_dimension=0, tiled=True)  91.3 us
    reduce_scatter x1, waiting for transfers between devices, per_device(): lax.psum_scatter(grad_feed_gate, 'dp', scatter_dimension=0, tiled=True)  91.3 us
    dot_general x8, matrix products, contract_rows(): lax.dot_general(left_mat, right_mat, (((0,), (0,)), ((), ())), preferred_...  67.1 us
    dot_general x8, matrix products, times_transposed(): lax.dot_general(left_mat, right_mat, (((1,), (1,)), ((), ())), preferred_...  64.4 us
  transfers between devices with their start and end apart: 18, of which 15 were waited for; matrix products, arithmetic and copies ran while one was open for 9% of the time, Pallas kernels for 0%

profile of v1, /device:TPU:0, one launch (start us, length us, event | category | flops | bytes accessed | tf_op | source)
XLA Modules:
  0.0 2241.7 jit_solution(4217456859577839967)
XLA Ops:
  11.7 10.5 scatter_custom_fusion.1
  22.2 5.3 all-to-all-start
  30.1 19.2 scatter_custom_fusion
  50.7 26.0 %all-to-all-done = bf16[8,128,2048]{2,1,0:T(8,128)(2,1)} async-done(((bf16[8,128,2048]{2,1,0:T(8,128)(2,1)}), bf16[8,128,2048]{2,1,0:T(8,128)(2,1)}, u32[]{:S(2)}, u32[]{:S(2)}) %all-to-all-start) | async-done | bytes 4194336 | tf_op jit(solution)/shard_map/all_to_all | solution.py:129
  76.7 10.2 scatter_custom_fusion.2
  109.1 6.7 fusion.66
  120.2 61.7 %while.36 = (s32[]{:T(128)}, f32[256,512]{1,0:T(8,128)S(1)}, f32[16,256,512]{2,1,0:T(8,128)}, f32[16,256]{1,0:T(8,128)S(1)}, f32[16,256,1]{1,2,0:T(1,128)}, /*in...) while((s32[]{:T(128)}, f32[256,512]{1,0:T(8,128)S(1)}, ...), condition=%wide.region_13.14_spmd.clone, body=%wide.region_12.13_spmd.clone.sunk | while | flops 524547 | bytes 2629268 | solution.py:62
  181.9 10.8 multiply_reduce_fusion.4
  192.9 6.9 multiply_convert_fusion.4
  200.8 5.6 fusion.85
  206.4 10.9 scatter_custom_fusion.3
  217.3 4.7 all-to-all-start.2
  222.1 49.1 %all-to-all-done.2 = bf16[8,128,2048]{2,1,0:T(8,128)(2,1)} async-done(((bf16[8,128,2048]{2,1,0:T(8,128)(2,1)}), bf16[8,128,2048]{2,1,0:T(8,128)(2,1)}, u32[]{:S(2)}, u32[]{:S(2)}) %all-to-all-start.2) | async-done | bytes 4194336 | tf_op jit(solution)/shard_map/all_to_all | solution.py:130
  271.1 10.1 scatter_custom_fusion.4
  281.3 216.3 %all-reduce.13.cloned.1.call-done = f32[1024,2048]{1,0:T(8,128)} async-done(((f32[1024,2048]{1,0:T(8,128)}), f32[1024,2048]{1,0:T(8,128)}) %all-reduce.13.cloned.1.call-update) | async-done | bytes 8388624 | tf_op jit(solution)/shard_map/psum | solution.py:193
  497.5 5.5 multiply_reduce_fusion.2
  506.3 11.8 fusion.87
  518.1 10.3 fusion.86
  528.5 15.1 multiply_convert_fusion.1
  543.6 9.7 fusion.88
  553.3 10.8 convolution_add_fusion.1
  564.2 10.9 convolution_convert_fusion
  575.2 279.0 %all-reduce.15.cloned.1.call-done = f32[1024,2048]{1,0:T(8,128)} async-done(((f32[1024,2048]{1,0:T(8,128)}), f32[1024,2048]{1,0:T(8,128)}) %all-reduce.15.cloned.1.call-update) | async-done | bytes 8388624 | tf_op jit(solution)/shard_map/psum | solution.py:218
  854.2 8.0 multiply_reduce_fusion
  862.2 279.4 %all-gather.3.cloned.1.call-done = bf16[4096,2048]{1,0:T(8,128)(2,1)} async-done(((bf16[1024,2048]{1,0:T(8,128)(2,1)}), bf16[4096,2048]{1,0:T(8,128)(2,1)}) %all-gather.3.cloned.1.call-update) | async-done | bytes 16777232 | tf_op jit(solution)/shard_map/all_gather | solution.py:204
  1141.6 12.1 reduce_sum.157
  1153.7 12.5 fusion.6
  1166.3 6.9 multiply_reduce_fusion.3
  1179.8 9.8 fusion.57
  1191.3 9.4 fusion.34
  1200.7 5.7 fusion.92
  1210.8 78.7 %while.37 = (s32[]{:T(128)}, f32[256,512]{1,0:T(8,128)S(1)}, f32[16,256,512]{2,1,0:T(8,128)}, f32[16,256]{1,0:T(8,128)S(1)}, f32[16,256,512]{2,1,0:T(8,128)}, /*...) while((s32[]{:T(128)}, f32[256,512]{1,0:T(8,128)S(1)}, ...), condition=%wide.region_25.26_spmd.clone, body=%wide.region_23.25_spmd.clone.sunk | while | flops 786692 | bytes 3157176 | solution.py:62
  1289.6 8.5 fusion.62
  1298.2 5.9 add_convert_fusion.1
  1311.7 5.7 fusion.91
  1319.7 9.1 add_add_fusion.2
  1332.3 11.8 fusion.12
  1344.2 12.1 fusion.99
  1356.4 11.9 fusion.98
  1368.3 4.9 fusion.94
  1373.4 4.9 fusion.93
  1378.3 8.0 fusion.24
  1387.5 6.8 fusion.96
  1394.4 4.9 concatenate.10
  1399.2 11.8 gather_fusion
  1411.1 4.7 all-to-all-start.1
  1415.8 6.7 fusion.95
  1422.5 198.4 %all-reduce.17.cloned.1.call-done = (f32[1024,2048]{1,0:T(8,128)}, f32[1024,16]{0,1:T(8,128)}) async-done(((f32[1024,2048]{1,0:T(8,128)}, f32[1024,16]{0,1:T(8,128)}), (f32[1024,2048]{1,0:T(8,128)}, f32[1024,16]{0,1:T(8,128)})) %all-reduce.17.cloned.1.call-update) | async-done | bytes 8454160 | tf_op jit(solution)/shard_map/psum | solution.py:241
  1620.9 9.0 fusion.5
  1633.7 4.7 concatenate.11
  1638.5 11.6 gather_fusion.2
  1650.1 4.7 all-to-all-start.3
  1663.6 9.7 gather_fusion.1
  1673.3 61.1 %all-reduce.7 = (f32[2048]{0:T(1024)S(1)}, f32[256]{0:T(256)S(1)}, f32[512]{0:T(512)S(1)}, f32[2048]{0:T(1024)S(1)}) all-reduce(f32[2048]{0:T(1024)S(1)} %get-tuple-element.304, f32[256]{0:T(256)S(1)} %neg.53, f32[512]{0:T(512)S(1)} %copy-done.74, f32[2048]{0:T(1024)S(1)} %copy-done.66), channel_id=3, replica_groups=mesh['dp'=8,'tensor'=4] {'dp'}, use_global_device_ids=true, to_apply=%region_32.33.clone | all-reduce | flops 4864 | bytes 38912
  1735.7 8.8 psum.40
  1745.2 9.9 gather_fusion.3
  1758.8 91.3 %reduce-scatter.27.cloned.1.call-done = f32[256,1408]{1,0:T(8,128)} async-done(((f32[2048,1408]{1,0:T(8,128)}), f32[256,1408]{1,0:T(8,128)}) %reduce-scatter.27.cloned.1.call-update) | async-done | bytes 1441808 | tf_op jit(solution)/shard_map/reduce_scatter | solution.py:271
  1850.0 91.3 %reduce-scatter.25.cloned.1.call-done = f32[256,1408]{1,0:T(8,128)} async-done(((f32[2048,1408]{1,0:T(8,128)}), f32[256,1408]{1,0:T(8,128)}) %reduce-scatter.25.cloned.1.call-update) | async-done | bytes 1441808 | tf_op jit(solution)/shard_map/reduce_scatter | solution.py:270
  1941.3 45.4 %reduce-scatter.15.cloned.1.call-done = f32[256,256]{1,0:T(8,128)} async-done(((f32[2048,256]{1,0:T(8,128)}), f32[256,256]{1,0:T(8,128)}) %reduce-scatter.15.cloned.1.call-update) | async-done | bytes 262160 | tf_op jit(solution)/shard_map/reduce_scatter | solution.py:261
  1986.8 44.9 %reduce-scatter.13.cloned.1.call-done = f32[256,256]{1,0:T(8,128)} async-done(((f32[2048,256]{1,0:T(8,128)}), f32[256,256]{1,0:T(8,128)}) %reduce-scatter.13.cloned.1.call-update) | async-done | bytes 262160 | tf_op jit(solution)/shard_map/reduce_scatter | solution.py:260
  2031.7 55.7 %reduce-scatter.23.cloned.1.call-done = f32[64,2048]{1,0:T(8,128)} async-done(((f32[512,2048]{1,0:T(8,128)}), f32[64,2048]{1,0:T(8,128)}) %reduce-scatter.23.cloned.1.call-update) | async-done | bytes 524304 | tf_op jit(solution)/shard_map/reduce_scatter | solution.py:268
  2087.4 55.1 %reduce-scatter.19.cloned.1.call-done = f32[256,512]{1,0:T(8,128)} async-done(((f32[2048,512]{1,0:T(8,128)}), f32[256,512]{1,0:T(8,128)}) %reduce-scatter.19.cloned.1.call-update) | async-done | bytes 524304 | tf_op jit(solution)/shard_map/reduce_scatter | solution.py:263
  2142.5 55.7 %reduce-scatter.17.cloned.1.call-done = f32[256,512]{1,0:T(8,128)} async-done(((f32[2048,512]{1,0:T(8,128)}), f32[256,512]{1,0:T(8,128)}) %reduce-scatter.17.cloned.1.call-update) | async-done | bytes 524304 | tf_op jit(solution)/shard_map/reduce_scatter | solution.py:262
  2198.2 36.8 %reduce-scatter.21.cloned.1.call-done = f32[256,16]{0,1:T(8,128)} async-done(((f32[2048,16]{0,1:T(8,128)}), f32[256,16]{0,1:T(8,128)}) %reduce-scatter.21.cloned.1.call-update) | async-done | bytes 16400 | tf_op jit(solution)/shard_map/reduce_scatter | solution.py:264
  (509 shorter events, 221.9 us)
Async XLA Ops:
  7.2 185.7 %copy-start = (bf16[2048,512]{1,0:T(8,128)(2,1)S(1)}, bf16[2048,512]{1,0:T(8,128)(2,1)}, u32[]{:S(2)}) copy-start(bf16[2048,512]{1,0:T(8,128)(2,1)} %param.30) | copy-start | bytes 6291460
  11.7 194.7 %copy-start.68 = (s32[640]{0:T(1024)}, s32[640]{0:T(1024)S(1)}, u32[]{:S(2)}) copy-start(s32[640]{0:T(1024)S(1)} %compare_select_fusion.4) | copy-start | bytes 7684
  22.2 54.5 %all-to-all-start = ((bf16[8,128,2048]{2,1,0:T(8,128)(2,1)}), bf16[8,128,2048]{2,1,0:T(8,128)(2,1)}, u32[]{:S(2)}, u32[]{:S(2)}) async-start(bf16[8,128,2048]{2,1,0:T(8,128)(2,1)} %bitcast.201), calls=%async_computation | async-start | bytes 8388608 | tf_op jit(solution)/shard_map/all_to_all | solution.py:129
  27.5 470.0 %all-reduce.13.cloned.1.call-start = ((), (), s32[]{:S(2)}) async-start(), calls=%async_computation.14 | async-start | bytes 16777216 | tf_op jit(solution)/shard_map/psum | solution.py:193
  27.9 76.1 %copy-start.41 = (s32[16,64]{1,0:T(8,128)}, s32[16,64]{1,0:T(8,128)S(1)}, u32[]{:S(2)}) copy-start(s32[16,64]{1,0:T(8,128)S(1)} %eq.92) | copy-start | bytes 12292
  28.0 62.1 %copy-start.53 = (f32[2048]{0:T(1024)}, f32[2048]{0:T(1024)S(1)}, u32[]{:S(2)}) copy-start(f32[2048]{0:T(1024)S(1)} %convert_element_type.129) | copy-start | bytes 24580
  49.7 54.4 %copy-start.57 = (pred[64,64]{1,0:T(8,128)(4,1)}, pred[64,64]{1,0:T(8,128)(4,1)S(1)}, u32[]{:S(2)}) copy-start(pred[64,64]{1,0:T(8,128)(4,1)S(1)} %iota_compare_fusion) | copy-start | bytes 12292
  49.9 59.2 %copy-start.55 = (f32[16,64]{1,0:T(8,128)}, f32[16,64]{1,0:T(8,128)S(1)}, u32[]{:S(2)}) copy-start(f32[16,64]{1,0:T(8,128)S(1)} %get-tuple-element.369) | copy-start | bytes 12292
  49.9 132.0 %copy-start.50 = (f32[16,64]{1,0:T(8,128)}, f32[16,64]{1,0:T(8,128)S(1)}, u32[]{:S(2)}) copy-start(f32[16,64]{1,0:T(8,128)S(1)} %get-tuple-element.370) | copy-start | bytes 12292
  96.8 12.3 copy-start.12
  99.2 9.9 copy-start.15
  106.8 9.0 copy-start.19
  181.9 10.9 copy-start.43
  181.9 10.9 copy-start.67
  181.9 10.9 copy-start.76
  192.9 7.9 copy-start.78
  217.3 53.8 %all-to-all-start.2 = ((bf16[8,128,2048]{2,1,0:T(8,128)(2,1)}), bf16[8,128,2048]{2,1,0:T(8,128)(2,1)}, u32[]{:S(2)}, u32[]{:S(2)}) async-start(bf16[8,128,2048]{2,1,0:T(8,128)(2,1)} %bitcast.202), calls=%async_computation.2 | async-start | bytes 8388608 | tf_op jit(solution)/shard_map/all_to_all | solution.py:130
  222.0 632.2 %all-reduce.15.cloned.1.call-start = ((), (), s32[]{:S(2)}) async-start(), calls=%async_computation.15 | async-start | bytes 16777216 | tf_op jit(solution)/shard_map/psum | solution.py:218
  506.3 11.8 copy-start.23
  506.3 22.1 slice-start.6
  518.1 10.3 slice-start.7
  543.6 9.8 copy-start.84
  564.2 577.4 %all-gather.3.cloned.1.call-start = ((), (), s32[]{:S(2)}) async-start(), calls=%async_computation.25 | async-start | bytes 20971520 | tf_op jit(solution)/shard_map/all_gather | solution.py:204
  575.2 1045.7 %all-reduce.17.cloned.1.call-start = ((), (), s32[]{:S(2)}) async-start(), calls=%async_computation.27 | async-start | bytes 16908288 | tf_op jit(solution)/shard_map/psum | solution.py:241
  1153.7 12.5 copy-start.18
  1153.7 12.5 copy-start.30
  1175.2 25.5 %copy-start.34 = (bf16[1024,512]{1,0:T(8,128)(2,1)}, bf16[1024,512]{1,0:T(8,128)(2,1)S(1)}, u32[]{:S(2)}) copy-start(bf16[1024,512]{1,0:T(8,128)(2,1)S(1)} %get-tuple-element.363) | copy-start | bytes 3145732
  1175.2 16.1 slice-start.2
  1176.4 13.2 copy-start.21
  1179.8 9.8 copy-start.6
  1179.8 9.8 copy-start.13
  1179.8 11.5 slice-start.3
  1210.8 78.8 %copy-start.14 = (bf16[1024,256]{1,0:T(8,128)(2,1)S(1)}, bf16[1024,256]{1,0:T(8,128)(2,1)}, u32[]{:S(2)}) copy-start(bf16[1024,256]{1,0:T(8,128)(2,1)} %copy-done.12) | copy-start | bytes 1572868
  1210.8 78.8 %copy-start.44 = (f32[16,256]{1,0:T(8,128)S(1)}, f32[16,256]{1,0:T(8,128)}, u32[]{:S(2)}) copy-start(f32[16,256]{1,0:T(8,128)} %copy-done.43) | copy-start | bytes 49156
  1210.8 78.8 %copy-start.56 = (f32[16,64]{1,0:T(8,128)S(1)}, f32[16,64]{1,0:T(8,128)}, u32[]{:S(2)}) copy-start(f32[16,64]{1,0:T(8,128)} %copy-done.55) | copy-start | bytes 12292
  1289.6 8.6 copy-start.3
  1289.6 8.6 copy-start.17
  1304.1 7.6 copy-start.39
  1307.2 10.2 copy-start.27
  1328.9 333.3 %reduce-scatter.31.cloned.1.call-start = ((), (), s32[]{:S(2)}) async-start(), calls=%async_computation.26 | async-start | bytes 147456
  1332.2 426.6 %reduce-scatter.29.cloned.1.call-start = ((), (), s32[]{:S(2)}) async-start(), calls=%async_computation.24 | async-start | bytes 12976128 | tf_op jit(solution)/shard_map/reduce_scatter | solution.py:272
  1344.1 505.9 %reduce-scatter.27.cloned.1.call-start = ((), (), s32[]{:S(2)}) async-start(), calls=%async_computation.23 | async-start | bytes 12976128 | tf_op jit(solution)/shard_map/reduce_scatter | solution.py:271
  1356.4 585.0 %reduce-scatter.25.cloned.1.call-start = ((), (), s32[]{:S(2)}) async-start(), calls=%async_computation.22 | async-start | bytes 12976128 | tf_op jit(solution)/shard_map/reduce_scatter | solution.py:270
  1368.3 618.5 %reduce-scatter.15.cloned.1.call-start = ((), (), s32[]{:S(2)}) async-start(), calls=%async_computation.17 | async-start | bytes 2359296 | tf_op jit(solution)/shard_map/reduce_scatter | solution.py:261
  1373.3 658.4 %reduce-scatter.13.cloned.1.call-start = ((), (), s32[]{:S(2)}) async-start(), calls=%async_computation.16 | async-start | bytes 2359296 | tf_op jit(solution)/shard_map/reduce_scatter | solution.py:260
  1378.3 709.1 %reduce-scatter.23.cloned.1.call-start = ((), (), s32[]{:S(2)}) async-start(), calls=%async_computation.21 | async-start | bytes 4718592 | tf_op jit(solution)/shard_map/reduce_scatter | solution.py:268
  1386.3 756.2 %reduce-scatter.19.cloned.1.call-start = ((), (), s32[]{:S(2)}) async-start(), calls=%async_computation.19 | async-start | bytes 4718592 | tf_op jit(solution)/shard_map/reduce_scatter | solution.py:263
  1411.1 239.0 %all-to-all-start.1 = ((bf16[8,128,2048]{2,1,0:T(8,128)(2,1)}), bf16[8,128,2048]{2,1,0:T(8,128)(2,1)}, u32[]{:S(2)}, u32[]{:S(2)}) async-start(bf16[8,128,2048]{2,1,0:T(8,128)(2,1)} %bitcast.199), calls=%async_computation.1 | async-start | bytes 8388608 | tf_op jit(solution)/shard_map/all_to_all | solution.py:275
  1415.8 782.4 %reduce-scatter.17.cloned.1.call-start = ((), (), s32[]{:S(2)}) async-start(), calls=%async_computation.18 | async-start | bytes 4718592 | tf_op jit(solution)/shard_map/reduce_scatter | solution.py:262
  1415.8 214.1 %slice-start = ((s8[4227072]{0:T(1024)(128)(4,1)}), s8[32768]{0:T(1024)(128)(4,1)S(1)}, s32[]{:S(2)}) async-start(s8[4227072]{0:T(1024)(128)(4,1)} %bitcast.177), calls=%async_computation.28 | async-start | bytes 65536
  1422.5 198.4 %copy-start.48 = (bf16[2048,16]{0,1:T(8,128)(2,1)S(1)}, bf16[2048,16]{0,1:T(8,128)(2,1)}, u32[]{:S(2)}) copy-start(bf16[2048,16]{0,1:T(8,128)(2,1)} %param.31) | copy-start | bytes 196612
  1422.5 198.4 %copy-start.54 = (f32[2048]{0:T(1024)S(1)}, f32[2048]{0:T(1024)}, u32[]{:S(2)}) copy-start(f32[2048]{0:T(1024)} %copy-done.53) | copy-start | bytes 24580
  1422.5 198.4 %copy-start.60 = (f32[1024]{0:T(1024)S(1)}, f32[1024]{0:T(1024)}, u32[]{:S(2)}) copy-start(f32[1024]{0:T(1024)} %copy-done.59) | copy-start | bytes 12292
  1620.9 9.1 slice-start.4
  1620.9 9.0 copy-start.63
  1620.9 9.1 slice-start.1
  1620.9 9.1 slice-start.5
  1650.1 7.5 copy-start.49
  1650.1 95.1 %all-to-all-start.3 = ((bf16[8,128,2048]{2,1,0:T(8,128)(2,1)}), bf16[8,128,2048]{2,1,0:T(8,128)(2,1)}, u32[]{:S(2)}, u32[]{:S(2)}) async-start(bf16[8,128,2048]{2,1,0:T(8,128)(2,1)} %bitcast.198), calls=%async_computation.3 | async-start | bytes 8388608 | tf_op jit(solution)/shard_map/all_to_all | solution.py:276
  1654.8 7.4 copy-start.69
  1654.8 580.2 %reduce-scatter.21.cloned.1.call-start = ((), (), s32[]{:S(2)}) async-start(), calls=%async_computation.20 | async-start | bytes 147456 | tf_op jit(solution)/shard_map/reduce_scatter | solution.py:264
  1663.6 9.7 copy-start.66
  1663.6 9.7 copy-start.74
  1745.2 489.8 %copy-start.1 = (bf16[2048,512]{1,0:T(8,128)(2,1)S(1)}, bf16[2048,512]{1,0:T(8,128)(2,1)}, u32[]{:S(2)}) copy-start(bf16[2048,512]{1,0:T(8,128)(2,1)} %param.30) | copy-start | bytes 6291460
  (49 other events, 201.3 us)
Sparse Core Ops, SparseCore 0:
  206.5 290.9 all-reduce.12
  564.3 289.8 all-reduce.14
  855.8 285.7 all-gather.2
  1329.0 291.8 all-reduce.16
  1623.7 32.3 reduce-scatter.30
  1660.5 98.2 reduce-scatter.28
  1763.3 86.7 reduce-scatter.26
  1854.5 86.7 reduce-scatter.24
  1945.5 41.1 reduce-scatter.14
  1990.5 41.1 reduce-scatter.12
  2036.0 51.3 reduce-scatter.22
  2091.2 51.2 reduce-scatter.18
  2146.8 51.3 reduce-scatter.16
  2201.6 33.3 reduce-scatter.20
